TPU v7x, 512 devices: a whole 4x8x8 slice. The times are simulated.
512 devices in a mesh: lon: 32 (over x, y), lat: 4 (over z_lo, core), lev: 4 (over z_hi).
Axes of the slice: x: 4, y: 8, z: 8 (z_hi: 4, z_lo: 2; z = z_hi * 2 + z_lo), core: 2. Of those that a mesh axis runs over, the one named last changes fastest.
Arguments:
- adjoint_field: float32 [12, 12, 128, 4096], P(None, 'lev', 'lat', 'lon'), may hold values from -6 to 6
- east_courant: float32 [12, 128, 4096], P('lev', 'lat', 'lon'), may hold values from -0.2 to 0.2
- north_courant: float32 [12, 128, 4096], P('lev', 'lat', 'lon'), may hold values from -0.2 to 0.2
- pole_courant: float32 [12, 4096], P('lev', 'lon'), may hold values from -0.2 to 0.2
- mix_fraction: float32 [12, 128, 4096], P('lev', 'lat', 'lon'), may hold values from 0.05 to 0.6
- detrain_share: float32 [12, 128, 4096], P('lev', 'lat', 'lon'), may hold values from 0.1 to 3
- sounding_owner: int32 [2, 32768, 1], P(None, ('lon', 'lat')), may hold values from 0 to 127; in each aligned block of 256 rows (0 to 255, 256 to 511, ..., all dimensions but the last counted through in order) at most 4 rows name the same one
- sounding_cell: int32 [2, 32768], P(None, ('lon', 'lat')), may hold values from 0 to 4095
- sounding_count: int32 [2, 128], P(None, ('lon', 'lat')), may hold values from 1 to 256, 20480 in all within a row
- sounding_forcing: float32 [2, 12, 32768], P(None, 'lev', ('lon', 'lat')), may hold values from -6 to 6
Outputs:
- earlier_adjoint: float32 [12, 12, 128, 4096], P(None, 'lev', 'lat', 'lon')
Inputs may be any that keep to these rules, and one draw needn't show every extreme that they name: `sounding_owner`: in each aligned block of 256 slots of one step (the slots of one device) no owner is named more than 4 times, a bound that some block reaches. `sounding_count`: each step's counts sum to 20480; at each step some device has exactly 256.
All inputs are finite; a program needn't handle non-finite values.
Results may differ from a plain program's by a relative error of at most 0.0001.
Values sent between devices are 32-bit elements; how exact they have to be, the bound alone decides.
A program may use at most 128 MiB of HBM per device.

v0:
```python
import jax
import jax.numpy as jnp
from jax import lax
from jax.sharding import PartitionSpec as P


def from_behind(value, axis, steps):
    count = lax.axis_size(axis)
    pairs = [(source, (source + steps) % count) for source in range(count)]
    return lax.ppermute(value, axis, pairs)


def from_behind_2(block, axis, distance):
    devices = range(lax.axis_size(axis))
    route = [(i - distance, i) for i in devices if i - distance in devices]
    return lax.ppermute(block, axis, route)


def extended(x, sides, width, wrap):
    for axis, dim in sides:
        size, length = (lax.axis_size(axis), x.shape[dim])
        up = [(i, (i + 1) % size) for i in range(size if wrap else size - 1)]
        down = [(j, i) for i, j in up]
        last = lax.slice_in_dim(x, length - width, length, axis=dim)
        initial = lax.slice_in_dim(x, 0, width, axis=dim)
        before = lax.ppermute(last, axis, up)
        after = lax.ppermute(initial, axis, down)
        x = jnp.concatenate([before, x, after], axis=dim)
    return x


def mix_sum(partial_sum):
    return lax.psum(partial_sum, "lev")


def on_device(
    adjoint_field,
    east_courant,
    north_courant,
    pole_courant,
    mix_fraction,
    detrain_share,
    sounding_owner,
    sounding_cell,
    sounding_count,
    sounding_forcing,
):
    lon_count = lax.axis_size("lon")
    lat_count = lax.axis_size("lat")
    lat_place = lax.axis_index("lat")
    owner_self = lax.axis_index("lon") * lat_count + lat_place
    tracers, lev_dev, lat_rows, lon_cols = adjoint_field.shape
    step_count = sounding_forcing.shape[0]
    slot_count = sounding_forcing.shape[2]
    grid_cells = lat_rows * lon_cols
    owner_count = lon_count * lat_count
    cap = 4
    live_slots = jnp.arange(slot_count, dtype=jnp.int32)[None, :] < sounding_count
    values = jnp.where(live_slots[:, None, :], sounding_forcing, 0.0)
    owner_ids = sounding_owner[:, :, 0]
    slot_iota = jnp.arange(slot_count, dtype=jnp.int32)
    earlier = slot_iota[None, :, None] < slot_iota[None, None, :]
    same_owner = owner_ids[:, :, None] == owner_ids[:, None, :]
    rank = jnp.sum(jnp.logical_and(earlier, same_owner), axis=1, dtype=jnp.int32)
    position = owner_ids * cap + rank
    bucket_iota = jnp.arange(owner_count * cap, dtype=jnp.int32)
    chosen = position[:, :, None] == bucket_iota[None, None, :]
    bucket_values = jnp.sum(jnp.where(chosen[:, None, :, :], values[:, :, :, None], 0.0), axis=2)
    bucket_cell = (
        jnp.max(jnp.where(chosen, sounding_cell[:, :, None] + 1, 0), axis=1).astype(jnp.float32)
        - 1.0
    )
    packed = jnp.concatenate([bucket_values, bucket_cell[:, None, :]], axis=1)
    packed = packed.reshape(step_count, lev_dev + 1, owner_count, cap)
    packed = jnp.transpose(packed, (2, 0, 1, 3))
    arrived = lax.all_to_all(packed, ("lon", "lat"), 0, 0, tiled=True)
    arrived = jnp.transpose(arrived, (1, 2, 0, 3)).reshape(
        step_count, lev_dev + 1, owner_count * cap
    )
    cell_iota = jnp.arange(grid_cells, dtype=jnp.int32).astype(jnp.float32)
    hit = (arrived[:, lev_dev, :, None] == cell_iota[None, None, :]).astype(jnp.float32)
    forcing_grid = jnp.einsum(
        "tke,tec->tkc", arrived[:, :lev_dev, :], hit, precision=lax.Precision.HIGHEST
    )
    forcing_grid = forcing_grid.reshape(step_count, lev_dev, lat_rows, lon_cols)
    west_column = from_behind(east_courant[:, :, -1:], "lon", 1)
    west_wind = jnp.concatenate([west_column, east_courant[:, :, :-1]], axis=2)
    south_row = from_behind_2(north_courant[:, -1:, :], "lat", 1)
    south_wind = jnp.concatenate([south_row, north_courant[:, :-1, :]], axis=1)
    pole_pair = jnp.stack([north_courant[:, -1, :], pole_courant], axis=0)
    partner_winds = from_behind(pole_pair, "lon", lon_count // 2)
    row_index = jnp.arange(lat_rows, dtype=jnp.int32)[None, :, None]
    at_top = jnp.logical_and(lat_place == lat_count - 1, row_index == lat_rows - 1)
    at_bottom = jnp.logical_and(lat_place == 0, row_index == 0)
    upwind_east = jnp.maximum(east_courant, 0.0)
    upwind_west = -jnp.minimum(west_wind, 0.0)
    upwind_north = jnp.maximum(north_courant, 0.0) + jnp.where(
        at_top, -jnp.minimum(partner_winds[0], 0.0)[:, None, :], 0.0
    )
    upwind_south = jnp.where(
        at_bottom,
        (jnp.maximum(pole_courant, 0.0) - jnp.minimum(partner_winds[1], 0.0))[:, None, :],
        -jnp.minimum(south_wind, 0.0),
    )
    total_detrain = lax.psum(jnp.sum(detrain_share, axis=0), "lev")
    adjoint = adjoint_field
    for position in range(step_count):
        step_now = step_count - 1 - position
        adjoint = adjoint + forcing_grid[step_now][None]
        partial_sum = jnp.sum(detrain_share[None] * adjoint, axis=1)
        column_sum = mix_sum(partial_sum)
        adjoint = (1.0 - mix_fraction)[None] * adjoint + mix_fraction[None] * (
            column_sum / total_detrain
        )[:, None]
        across = extended(adjoint, (("lon", 3),), 1, True)
        east_side = across[:, :, :, 2:]
        west_side = across[:, :, :, :-2]
        upright = extended(adjoint, (("lat", 2),), 1, False)
        north_side = upright[:, :, 2:, :]
        south_side = upright[:, :, :-2, :]
        edge_row = jnp.where(lat_place == 0, adjoint[:, :, :1, :], adjoint[:, :, -1:, :])
        partner_row = from_behind(edge_row, "lon", lon_count // 2)
        north_side = jnp.where(at_top, partner_row, north_side)
        south_side = jnp.where(at_bottom, partner_row, south_side)
        adjoint = (
            adjoint
            + upwind_east * (east_side - adjoint)
            + upwind_west * (west_side - adjoint)
            + upwind_north * (north_side - adjoint)
            + upwind_south * (south_side - adjoint)
        )
    return adjoint


def solution(mesh):
    return jax.shard_map(
        on_device,
        mesh=mesh,
        in_specs=(
            P(None, "lev", "lat", "lon"),
            P("lev", "lat", "lon"),
            P("lev", "lat", "lon"),
            P("lev", "lon"),
            P("lev", "lat", "lon"),
            P("lev", "lat", "lon"),
            P(None, ("lon", "lat"), None),
            P(None, ("lon", "lat")),
            P(None, ("lon", "lat")),
            P(None, "lev", ("lon", "lat")),
        ),
        out_specs=P(None, "lev", "lat", "lon"),
        check_vma=False,
    )
```

profile of v0, /device:TPU:1, one launch (start us, length us, event | category | flops | bytes accessed | tf_op | source)
XLA Modules:
  0.0 237.8 jit_solution(9995370526051326967)
XLA Ops:
  6.5 0.7 slice.102
  7.2 5.4 %collective-permute-start.6 = (f32[3,1,128]{2,0,1:T(4,128)S(1)}, f32[3,1,128]{2,0,1:T(4,128)S(1)}, u32[]{:S(2)}, u32[]{:S(2)}) collective-permute-start(f32[3,1,128]{2,0,1:T(4,128)S(1)} %copy.79), channel_id=1, source_target_pairs={{0,4},{4,8},{8,12},{1,5},{5,9},{9,13},{2,6},{6,10},{10,14},{3,7},{... | collective-permute-start | bytes 4616 | tf_op jit(solution)/shard_map/ppermute | solution.py:16
  13.3 4.6 %collective-permute-start.3 = (f32[2,3,128]{2,1,0:T(4,128)S(1)}, f32[2,3,128]{2,1,0:T(4,128)S(1)}, u32[]{:S(2)}, u32[]{:S(2)}) collective-permute-start(f32[2,3,128]{2,1,0:T(4,128)S(1)} %pad_maximum_fusion.8), channel_id=1, source_target_pairs={{0,256},{16,272},{32,288},{48,304},{64,320},{80,336},{96,352},{112... | collective-permute-start | bytes 9224 | tf_op jit(solution)/shard_map/ppermute | solution.py:10
  18.0 0.9 slice.98
  18.8 3.2 %collective-permute-start.1 = (f32[3,32,1]{2,1,0:T(8,128)S(1)}, f32[3,32,1]{2,1,0:T(8,128)S(1)}, u32[]{:S(2)}, u32[]{:S(2)}) collective-permute-start(f32[3,32,1]{2,1,0:T(8,128)S(1)} %slice.98), channel_id=1, source_target_pairs={{0,16},{16,32},{32,48},{48,64},{64,80},{80,96},{96,112},{112,128},... | collective-permute-start | bytes 1160 | tf_op jit(solution)/shard_map/ppermute | solution.py:10
  22.1 0.7 iota_compare_fusion.2
  24.2 0.7 broadcast_select_fusion.2
  25.0 0.7 fusion.45
  27.2 1.2 copy.40
  28.4 8.7 %all-to-all-start = ((f32[128,2,4,4]{3,1,2,0:T(2,128)}), f32[128,2,4,4]{3,1,2,0:T(2,128)S(1)}, u32[]{:S(2)}, u32[]{:S(2)}) async-start(f32[128,2,4,4]{3,1,2,0:T(2,128)} %copy.40), calls=%async_computation | async-start | bytes 1048576 | tf_op jit(solution)/shard_map/all_to_all | solution.py:76
  37.2 21.4 %psum.22 = f32[32,128]{1,0:T(8,128)S(1)} all-reduce(f32[32,128]{1,0:T(8,128)S(1)} %reduce_sum.51), channel_id=1, replica_groups=mesh['lon'=32,'lat'=4,'lev'=4] {'lev'}, use_global_device_ids=true, to_apply=%region_6.7 | all-reduce | flops 4096 | bytes 32768 | tf_op jit(solution)/shard_map/psum | solution.py:105
  59.3 4.8 %fusion = f32[2,3,4096]{2,1,0:T(4,128)S(1)} fusion(f32[4096]{0:T(1024)S(1)} %iota_convert_fusion, f32[2,512]{1,0:T(2,128)S(1)} %bitcast.56, f32[2,4,512]{2,1,0:T(4,128)S(1)} %reshape.146), kind=kOutput, calls=%fused_computation | convolution fusion | flops 155189248 | bytes 135168 | tf_op jit(solution)/shard_map/tke,tec->tkc/dot_general | solution.py:82
  64.2 1.1 fusion.36
  65.4 56.0 %all-reduce.3.cloned.1.call-done = f32[12,32,128]{2,0,1:T(8,128)} async-done(((f32[12,32,128]{2,0,1:T(8,128)}), f32[12,32,128]{2,0,1:T(8,128)}) %all-reduce.3.cloned.1.call-update) | async-done | bytes 196624 | tf_op jit(solution)/shard_map/psum | solution.py:33
  121.4 1.0 broadcast_divide_fusion.1
  123.8 4.6 %collective-permute-start.4 = (f32[12,3,1,128]{3,0,2,1:T(8,128)}, f32[12,3,1,128]{3,0,2,1:T(8,128)}, u32[]{:S(2)}, u32[]{:S(2)}) collective-permute-start(f32[12,3,1,128]{3,0,2,1:T(8,128)} %get-tuple-element.14), channel_id=1, source_target_pairs={{0,256},{16,272},{32,288},{48,304},{64,320},{80,336},{96,352},{112... | collective-permute-start | bytes 55304 | tf_op jit(solution)/shard_map/ppermute | solution.py:10
  128.3 5.3 %collective-permute-start.7 = (f32[12,3,1,128]{3,0,2,1:T(8,128)}, f32[12,3,1,128]{3,0,2,1:T(8,128)}, u32[]{:S(2)}, u32[]{:S(2)}) collective-permute-start(f32[12,3,1,128]{3,0,2,1:T(8,128)} %get-tuple-element.15), channel_id=1, source_target_pairs={{0,4},{4,8},{8,12},{1,5},{5,9},{9,13},{2,6},{6,10},{10,14},{3,7},{... | collective-permute-start | bytes 55304 | tf_op jit(solution)/shard_map/ppermute | solution.py:26
  133.7 2.1 collective-permute-start.5
  136.4 3.1 %collective-permute-start.2 = (f32[12,3,32,1]{2,3,1,0:T(1,128)S(1)}, f32[12,3,32,1]{2,3,1,0:T(1,128)S(1)}, u32[]{:S(2)}, u32[]{:S(2)}) collective-permute-start(f32[12,3,32,1]{2,3,1,0:T(1,128)S(1)} %copy.45), channel_id=1, source_target_pairs={{0,16},{16,32},{32,48},{48,64},{64,80},{80,96},{96,112},{112,128},... | collective-permute-start | bytes 13832 | tf_op jit(solution)/shard_map/ppermute | solution.py:26
  139.6 5.5 %collective-permute-start = (f32[12,3,32,1]{2,3,1,0:T(1,128)S(1)}, f32[12,3,32,1]{2,3,1,0:T(1,128)S(1)}, u32[]{:S(2)}, u32[]{:S(2)}) collective-permute-start(f32[12,3,32,1]{2,3,1,0:T(1,128)S(1)} %copy.43), channel_id=1, source_target_pairs={{16,0},{32,16},{48,32},{64,48},{80,64},{96,80},{112,96},{128,112},... | collective-permute-start | bytes 13832 | tf_op jit(solution)/shard_map/ppermute | solution.py:27
  145.2 0.8 collective-permute-done
  146.8 2.3 multiply_reduce_fusion
  149.2 52.8 %all-reduce.5.cloned.1.call-done = f32[12,32,128]{2,0,1:T(8,128)} async-done(((f32[12,32,128]{2,0,1:T(8,128)}), f32[12,32,128]{2,0,1:T(8,128)}) %all-reduce.5.cloned.1.call-update) | async-done | bytes 196624 | tf_op jit(solution)/shard_map/psum | solution.py:33
  201.9 1.0 broadcast_divide_fusion
  203.1 4.6 %collective-permute-start.10 = (f32[12,3,1,128]{3,0,2,1:T(8,128)S(1)}, f32[12,3,1,128]{3,0,2,1:T(8,128)S(1)}, u32[]{:S(2)}, u32[]{:S(2)}) collective-permute-start(f32[12,3,1,128]{3,0,2,1:T(8,128)S(1)} %get-tuple-element.7), channel_id=1, source_target_pairs={{0,256},{16,272},{32,288},{48,304},{64,320},{80,336},{96,352},{112... | collective-permute-start | bytes 55304 | tf_op jit(solution)/shard_map/ppermute | solution.py:10
  207.6 5.3 %collective-permute-start.12 = (f32[12,3,1,128]{3,0,2,1:T(8,128)S(1)}, f32[12,3,1,128]{3,0,2,1:T(8,128)S(1)}, u32[]{:S(2)}, u32[]{:S(2)}) collective-permute-start(f32[12,3,1,128]{3,0,2,1:T(8,128)S(1)} %get-tuple-element.8), channel_id=1, source_target_pairs={{0,4},{4,8},{8,12},{1,5},{5,9},{9,13},{2,6},{6,10},{10,14},{3,7},{... | collective-permute-start | bytes 55304 | tf_op jit(solution)/shard_map/ppermute | solution.py:26
  213.0 1.9 collective-permute-start.11
  215.5 5.1 %collective-permute-start.8 = (f32[12,3,32,1]{2,3,1,0:T(1,128)S(1)}, f32[12,3,32,1]{2,3,1,0:T(1,128)S(1)}, u32[]{:S(2)}, u32[]{:S(2)}) collective-permute-start(f32[12,3,32,1]{2,3,1,0:T(1,128)S(1)} %copy.49), channel_id=1, source_target_pairs={{16,0},{32,16},{48,32},{64,48},{80,64},{96,80},{112,96},{128,112},... | collective-permute-start | bytes 13832 | tf_op jit(solution)/shard_map/ppermute | solution.py:27
  220.9 1.9 collective-permute-start.9
  223.3 5.5 %collective-permute-done.9 = f32[12,3,32,1]{2,3,1,0:T(1,128)S(1)} collective-permute-done((f32[12,3,32,1]{2,3,1,0:T(1,128)S(1)}, f32[12,3,32,1]{2,3,1,0:T(1,128)S(1)}, u32[]{:S(2)}, u32[]{:S(2)}) %collective-permute-start.9) | collective-permute-done | bytes 4640 | tf_op jit(solution)/shard_map/ppermute | solution.py:26
  229.2 0.8 fusion.7
  230.0 1.0 copy.53
  (83 shorter events, 9.3 us)
Async XLA Ops:
  7.2 51.5 %collective-permute-start.6 = (f32[3,1,128]{2,0,1:T(4,128)S(1)}, f32[3,1,128]{2,0,1:T(4,128)S(1)}, u32[]{:S(2)}, u32[]{:S(2)}) collective-permute-start(f32[3,1,128]{2,0,1:T(4,128)S(1)} %copy.79), channel_id=1, source_target_pairs={{0,4},{4,8},{8,12},{1,5},{5,9},{9,13},{2,6},{6,10},{10,14},{3,7},{... | collective-permute-start | bytes 4616 | tf_op jit(solution)/shard_map/ppermute | solution.py:16
  13.3 45.5 %collective-permute-start.3 = (f32[2,3,128]{2,1,0:T(4,128)S(1)}, f32[2,3,128]{2,1,0:T(4,128)S(1)}, u32[]{:S(2)}, u32[]{:S(2)}) collective-permute-start(f32[2,3,128]{2,1,0:T(4,128)S(1)} %pad_maximum_fusion.8), channel_id=1, source_target_pairs={{0,256},{16,272},{32,288},{48,304},{64,320},{80,336},{96,352},{112... | collective-permute-start | bytes 9224 | tf_op jit(solution)/shard_map/ppermute | solution.py:10
  18.8 39.8 %collective-permute-start.1 = (f32[3,32,1]{2,1,0:T(8,128)S(1)}, f32[3,32,1]{2,1,0:T(8,128)S(1)}, u32[]{:S(2)}, u32[]{:S(2)}) collective-permute-start(f32[3,32,1]{2,1,0:T(8,128)S(1)} %slice.98), channel_id=1, source_target_pairs={{0,16},{16,32},{32,48},{48,64},{64,80},{80,96},{96,112},{112,128},... | collective-permute-start | bytes 1160 | tf_op jit(solution)/shard_map/ppermute | solution.py:10
  28.4 8.7 %copy-start.2 = (f32[3,32,128]{2,1,0:T(8,128)S(1)}, f32[3,32,128]{2,1,0:T(8,128)}, u32[]{:S(2)}) copy-start(f32[3,32,128]{2,1,0:T(8,128)} %param.11) | copy-start | bytes 147460
  28.4 8.8 %copy-start.3 = (f32[3,32,128]{2,1,0:T(8,128)S(1)}, f32[3,32,128]{2,1,0:T(8,128)}, u32[]{:S(2)}) copy-start(f32[3,32,128]{2,1,0:T(8,128)} %param.14) | copy-start | bytes 147460
  28.4 8.8 %copy-start.1 = (f32[3,32,128]{2,1,0:T(8,128)S(1)}, f32[3,32,128]{2,1,0:T(8,128)}, u32[]{:S(2)}) copy-start(f32[3,32,128]{2,1,0:T(8,128)} %param.15) | copy-start | bytes 147460
  28.4 30.4 %copy-start.4 = (f32[3,32,128]{2,1,0:T(8,128)S(1)}, f32[3,32,128]{2,1,0:T(8,128)}, u32[]{:S(2)}) copy-start(f32[3,32,128]{2,1,0:T(8,128)} %param.12) | copy-start | bytes 147460
  28.4 30.5 %all-to-all-start = ((f32[128,2,4,4]{3,1,2,0:T(2,128)}), f32[128,2,4,4]{3,1,2,0:T(2,128)S(1)}, u32[]{:S(2)}, u32[]{:S(2)}) async-start(f32[128,2,4,4]{3,1,2,0:T(2,128)} %copy.40), calls=%async_computation | async-start | bytes 1048576 | tf_op jit(solution)/shard_map/all_to_all | solution.py:76
  37.1 84.3 %all-reduce.3.cloned.1.call-start = ((), (), s32[]{:S(2)}) async-start(), calls=%async_computation.1 | async-start | bytes 524288 | tf_op jit(solution)/shard_map/psum | solution.py:33
  37.2 26.9 %copy-start.7 = (pred[32]{0:T(512)(128)(4,1)}, pred[32]{0:T(512)(128)(4,1)S(1)}, u32[]{:S(2)}) copy-start(pred[32]{0:T(512)(128)(4,1)S(1)} %get-tuple-element.22) | copy-start | bytes 100
  37.2 107.8 %copy-start.5 = (pred[32]{0:T(512)(128)(4,1)}, pred[32]{0:T(512)(128)(4,1)S(1)}, u32[]{:S(2)}) copy-start(pred[32]{0:T(512)(128)(4,1)S(1)} %get-tuple-element.21) | copy-start | bytes 100
  59.3 4.8 %copy-start = (f32[12,3,32,128]{3,2,1,0:T(8,128)S(1)}, f32[12,3,32,128]{3,2,1,0:T(8,128)}, u32[]{:S(2)}) copy-start(f32[12,3,32,128]{3,2,1,0:T(8,128)} %param.10) | copy-start | bytes 1769476
  64.1 1.2 copy-start.9
  65.3 136.6 %all-reduce.5.cloned.1.call-start = ((), (), s32[]{:S(2)}) async-start(), calls=%async_computation.2 | async-start | bytes 524288 | tf_op jit(solution)/shard_map/psum | solution.py:33
  123.8 23.0 %collective-permute-start.4 = (f32[12,3,1,128]{3,0,2,1:T(8,128)}, f32[12,3,1,128]{3,0,2,1:T(8,128)}, u32[]{:S(2)}, u32[]{:S(2)}) collective-permute-start(f32[12,3,1,128]{3,0,2,1:T(8,128)} %get-tuple-element.14), channel_id=1, source_target_pairs={{0,256},{16,272},{32,288},{48,304},{64,320},{80,336},{96,352},{112... | collective-permute-start | bytes 55304 | tf_op jit(solution)/shard_map/ppermute | solution.py:10
  128.3 18.4 %collective-permute-start.7 = (f32[12,3,1,128]{3,0,2,1:T(8,128)}, f32[12,3,1,128]{3,0,2,1:T(8,128)}, u32[]{:S(2)}, u32[]{:S(2)}) collective-permute-start(f32[12,3,1,128]{3,0,2,1:T(8,128)} %get-tuple-element.15), channel_id=1, source_target_pairs={{0,4},{4,8},{8,12},{1,5},{5,9},{9,13},{2,6},{6,10},{10,14},{3,7},{... | collective-permute-start | bytes 55304 | tf_op jit(solution)/shard_map/ppermute | solution.py:26
  133.7 13.1 %collective-permute-start.5 = (f32[12,3,1,128]{3,0,2,1:T(8,128)}, f32[12,3,1,128]{3,0,2,1:T(8,128)}, u32[]{:S(2)}, u32[]{:S(2)}) collective-permute-start(f32[12,3,1,128]{3,0,2,1:T(8,128)} %get-tuple-element.16), channel_id=1, source_target_pairs={{4,0},{8,4},{12,8},{5,1},{9,5},{13,9},{6,2},{10,6},{14,10},{7,3},{... | collective-permute-start | bytes 55304 | tf_op jit(solution)/shard_map/ppermute | solution.py:27
  136.4 9.9 %collective-permute-start.2 = (f32[12,3,32,1]{2,3,1,0:T(1,128)S(1)}, f32[12,3,32,1]{2,3,1,0:T(1,128)S(1)}, u32[]{:S(2)}, u32[]{:S(2)}) collective-permute-start(f32[12,3,32,1]{2,3,1,0:T(1,128)S(1)} %copy.45), channel_id=1, source_target_pairs={{0,16},{16,32},{32,48},{48,64},{64,80},{80,96},{96,112},{112,128},... | collective-permute-start | bytes 13832 | tf_op jit(solution)/shard_map/ppermute | solution.py:26
  139.6 6.4 %collective-permute-start = (f32[12,3,32,1]{2,3,1,0:T(1,128)S(1)}, f32[12,3,32,1]{2,3,1,0:T(1,128)S(1)}, u32[]{:S(2)}, u32[]{:S(2)}) collective-permute-start(f32[12,3,32,1]{2,3,1,0:T(1,128)S(1)} %copy.43), channel_id=1, source_target_pairs={{16,0},{32,16},{48,32},{64,48},{80,64},{96,80},{112,96},{128,112},... | collective-permute-start | bytes 13832 | tf_op jit(solution)/shard_map/ppermute | solution.py:27
  203.1 26.1 %collective-permute-start.10 = (f32[12,3,1,128]{3,0,2,1:T(8,128)S(1)}, f32[12,3,1,128]{3,0,2,1:T(8,128)S(1)}, u32[]{:S(2)}, u32[]{:S(2)}) collective-permute-start(f32[12,3,1,128]{3,0,2,1:T(8,128)S(1)} %get-tuple-element.7), channel_id=1, source_target_pairs={{0,256},{16,272},{32,288},{48,304},{64,320},{80,336},{96,352},{112... | collective-permute-start | bytes 55304 | tf_op jit(solution)/shard_map/ppermute | solution.py:10
  207.6 21.5 %collective-permute-start.12 = (f32[12,3,1,128]{3,0,2,1:T(8,128)S(1)}, f32[12,3,1,128]{3,0,2,1:T(8,128)S(1)}, u32[]{:S(2)}, u32[]{:S(2)}) collective-permute-start(f32[12,3,1,128]{3,0,2,1:T(8,128)S(1)} %get-tuple-element.8), channel_id=1, source_target_pairs={{0,4},{4,8},{8,12},{1,5},{5,9},{9,13},{2,6},{6,10},{10,14},{3,7},{... | collective-permute-start | bytes 55304 | tf_op jit(solution)/shard_map/ppermute | solution.py:26
  213.0 16.2 %collective-permute-start.11 = (f32[12,3,1,128]{3,0,2,1:T(8,128)S(1)}, f32[12,3,1,128]{3,0,2,1:T(8,128)S(1)}, u32[]{:S(2)}, u32[]{:S(2)}) collective-permute-start(f32[12,3,1,128]{3,0,2,1:T(8,128)S(1)} %get-tuple-element.9), channel_id=1, source_target_pairs={{4,0},{8,4},{12,8},{5,1},{9,5},{13,9},{6,2},{10,6},{14,10},{7,3},{... | collective-permute-start | bytes 55304 | tf_op jit(solution)/shard_map/ppermute | solution.py:27
  215.5 7.3 %collective-permute-start.8 = (f32[12,3,32,1]{2,3,1,0:T(1,128)S(1)}, f32[12,3,32,1]{2,3,1,0:T(1,128)S(1)}, u32[]{:S(2)}, u32[]{:S(2)}) collective-permute-start(f32[12,3,32,1]{2,3,1,0:T(1,128)S(1)} %copy.49), channel_id=1, source_target_pairs={{16,0},{32,16},{48,32},{64,48},{80,64},{96,80},{112,96},{128,112},... | collective-permute-start | bytes 13832 | tf_op jit(solution)/shard_map/ppermute | solution.py:27
  220.9 8.3 %copy-start.6 = (pred[32]{0:T(512)(128)(4,1)S(1)}, pred[32]{0:T(512)(128)(4,1)}, u32[]{:S(2)}) copy-start(pred[32]{0:T(512)(128)(4,1)} %copy-done.5) | copy-start | bytes 100
  220.9 8.3 %copy-start.8 = (pred[32]{0:T(512)(128)(4,1)S(1)}, pred[32]{0:T(512)(128)(4,1)}, u32[]{:S(2)}) copy-start(pred[32]{0:T(512)(128)(4,1)} %copy-done.7) | copy-start | bytes 100
  220.9 7.8 %collective-permute-start.9 = (f32[12,3,32,1]{2,3,1,0:T(1,128)S(1)}, f32[12,3,32,1]{2,3,1,0:T(1,128)S(1)}, u32[]{:S(2)}, u32[]{:S(2)}) collective-permute-start(f32[12,3,32,1]{2,3,1,0:T(1,128)S(1)} %copy.51), channel_id=1, source_target_pairs={{0,16},{16,32},{32,48},{48,64},{64,80},{80,96},{96,112},{112,128},... | collective-permute-start | bytes 13832 | tf_op jit(solution)/shard_map/ppermute | solution.py:26
Sparse Core Ops, SparseCore 0:
  65.4 55.9 all-reduce.2
  149.3 52.6 all-reduce.4
where the time goes:
time: 239 us; the launch traced here: 238 us
  waiting for transfers between devices  115 us (48%)
  starting transfers between devices  61.3 us (26%)
  blocking collectives  21.4 us (9%)
  between operations  14 us (6%)
  other arithmetic  12.2 us (5%)
  local copies, waits for them, and re-layouts  9.05 us (4%)
  matrix products  4.78 us (2%)
    psum x2, waiting for transfers between devices, mix_sum(): return lax.psum(partial_sum, 'lev')  109 us
    psum x1, blocking collectives, on_device(): total_detrain = lax.psum(jnp.sum(detrain_share, axis=0), 'lev')  21.4 us
    ppermute x4, starting transfers between devices, from_behind(): return lax.ppermute(value, axis, pairs)  17 us
    ppermute x4, starting transfers between devices, extended(): before = lax.ppermute(last, axis, up)  15.6 us
    ppermute x4, starting transfers between devices, extended(): after = lax.ppermute(initial, axis, down)  14.6 us
    all_to_all x1, starting transfers between devices, on_device(): arrived = lax.all_to_all(packed, ('lon', 'lat'), 0, 0, tiled=True)  8.66 us
    ppermute x4, waiting for transfers between devices, extended(): before = lax.ppermute(last, axis, up)  5.48 us
    ppermute x1, starting transfers between devices, from_behind_2(): return lax.ppermute(block, axis, route)  5.38 us
  transfers between devices with their start and end apart: 16, of which 4 were waited for; matrix products, arithmetic and copies ran while one was open for 5% of the time, Pallas kernels for 0%

commit v1 on v0

--- a/solution.py
+++ b/solution.py
@@ -102,7 +102,7 @@
         (jnp.maximum(pole_courant, 0.0) - jnp.minimum(partner_winds[1], 0.0))[:, None, :],
         -jnp.minimum(south_wind, 0.0),
     )
-    total_detrain = lax.psum(jnp.sum(detrain_share, axis=0), "lev")
+    total_detrain = jnp.sum(lax.all_gather(jnp.sum(detrain_share, axis=0), "lev"), axis=0)
     adjoint = adjoint_field
     for position in range(step_count):
         step_now = step_count - 1 - position

time: 239 us -> 234 us (0.979)
  blocking collectives: 21.4 us -> 16.4 us
    psum x1 -> x0, blocking collectives: 21.4 us -> none  [on_device(): total_detrain = lax.psum(jnp.sum(detrain_share, axis=0), 'lev')]
    all_gather x0 -> x1, blocking collectives: none -> 16.4 us  [on_device(): lax.all_gather(jnp.sum(detrain_share, axis=0), 'lev')]
  transfers between devices with their start and end apart: 16 -> 16, of which waited for: 4 -> 5; matrix products, arithmetic and copies ran while one was open for 5% -> 5% of each run, Pallas kernels for 0% -> 0%
where the time goes in v1:
time: 234 us; the launch traced here: 233 us
  waiting for transfers between devices  115 us (49%)
  starting transfers between devices  61.3 us (26%)
  blocking collectives  16.4 us (7%)
  between operations  14 us (6%)
  other arithmetic  12.2 us (5%)
  local copies, waits for them, and re-layouts  9.05 us (4%)
  matrix products  4.78 us (2%)
    psum x2, waiting for transfers between devices, mix_sum(): return lax.psum(partial_sum, 'lev')  107 us
    ppermute x4, starting transfers between devices, from_behind(): return lax.ppermute(value, axis, pairs)  17 us
    all_gather x1, blocking collectives, on_device(): lax.all_gather(jnp.sum(detrain_share, axis=0), 'lev')  16.4 us
    ppermute x4, starting transfers between devices, extended(): before = lax.ppermute(last, axis, up)  15.6 us
    ppermute x4, starting transfers between devices, extended(): after = lax.ppermute(initial, axis, down)  14.6 us
    all_to_all x1, starting transfers between devices, on_device(): arrived = lax.all_to_all(packed, ('lon', 'lat'), 0, 0, tiled=True)  8.66 us
    ppermute x4, waiting for transfers between devices, extended(): before = lax.ppermute(last, axis, up)  5.48 us
    ppermute x1, starting transfers between devices, from_behind_2(): return lax.ppermute(block, axis, route)  5.38 us
  transfers between devices with their start and end apart: 16, of which 5 were waited for; matrix products, arithmetic and copies ran while one was open for 5% of the time, Pallas kernels for 0%

profile of v1, /device:TPU:1, one launch (start us, length us, event | category | flops | bytes accessed | tf_op | source)
XLA Modules:
  0.0 233.1 jit_solution(4173391218451256072)
XLA Ops:
  6.5 0.7 slice.102
  7.2 5.4 %collective-permute-start.6 = (f32[3,1,128]{2,0,1:T(4,128)S(1)}, f32[3,1,128]{2,0,1:T(4,128)S(1)}, u32[]{:S(2)}, u32[]{:S(2)}) collective-permute-start(f32[3,1,128]{2,0,1:T(4,128)S(1)} %copy.79), channel_id=1, source_target_pairs={{0,4},{4,8},{8,12},{1,5},{5,9},{9,13},{2,6},{6,10},{10,14},{3,7},{... | collective-permute-start | bytes 4616 | tf_op jit(solution)/shard_map/ppermute | solution.py:16
  13.3 4.6 %collective-permute-start.3 = (f32[2,3,128]{2,1,0:T(4,128)S(1)}, f32[2,3,128]{2,1,0:T(4,128)S(1)}, u32[]{:S(2)}, u32[]{:S(2)}) collective-permute-start(f32[2,3,128]{2,1,0:T(4,128)S(1)} %pad_maximum_fusion.8), channel_id=1, source_target_pairs={{0,256},{16,272},{32,288},{48,304},{64,320},{80,336},{96,352},{112... | collective-permute-start | bytes 9224 | tf_op jit(solution)/shard_map/ppermute | solution.py:10
  18.0 0.9 slice.98
  18.8 3.2 %collective-permute-start.1 = (f32[3,32,1]{2,1,0:T(8,128)S(1)}, f32[3,32,1]{2,1,0:T(8,128)S(1)}, u32[]{:S(2)}, u32[]{:S(2)}) collective-permute-start(f32[3,32,1]{2,1,0:T(8,128)S(1)} %slice.98), channel_id=1, source_target_pairs={{0,16},{16,32},{32,48},{48,64},{64,80},{80,96},{96,112},{112,128},... | collective-permute-start | bytes 1160 | tf_op jit(solution)/shard_map/ppermute | solution.py:10
  22.1 0.7 iota_compare_fusion.2
  24.2 0.7 broadcast_select_fusion.2
  25.0 0.7 fusion.45
  27.2 1.2 copy.40
  28.4 8.7 %all-to-all-start = ((f32[128,2,4,4]{3,1,2,0:T(2,128)}), f32[128,2,4,4]{3,1,2,0:T(2,128)S(1)}, u32[]{:S(2)}, u32[]{:S(2)}) async-start(f32[128,2,4,4]{3,1,2,0:T(2,128)} %copy.40), calls=%async_computation | async-start | bytes 1048576 | tf_op jit(solution)/shard_map/all_to_all | solution.py:76
  37.2 16.4 %all-gather = f32[128,128]{1,0:T(8,128)S(1)} all-gather(f32[32,128]{1,0:T(8,128)S(1)} %reduce_sum.60), channel_id=2, replica_groups=mesh['lon'=32,'lat'=4,'lev'=4] {'lev'}, dimensions={0}, use_global_device_ids=true | all-gather | bytes 81920 | tf_op jit(solution)/shard_map/all_gather | solution.py:105
  53.9 2.1 all-to-all-done
  56.4 4.8 %fusion = f32[2,3,4096]{2,1,0:T(4,128)S(1)} fusion(f32[4096]{0:T(1024)S(1)} %iota_convert_fusion, f32[2,512]{1,0:T(2,128)S(1)} %bitcast.58, f32[2,4,512]{2,1,0:T(4,128)S(1)} %reshape.146), kind=kOutput, calls=%fused_computation | convolution fusion | flops 155189248 | bytes 135168 | tf_op jit(solution)/shard_map/tke,tec->tkc/dot_general | solution.py:82
  61.3 1.1 fusion.36
  62.5 54.4 %all-reduce.3.cloned.1.call-done = f32[12,32,128]{2,0,1:T(8,128)} async-done(((f32[12,32,128]{2,0,1:T(8,128)}), f32[12,32,128]{2,0,1:T(8,128)}) %all-reduce.3.cloned.1.call-update) | async-done | bytes 196624 | tf_op jit(solution)/shard_map/psum | solution.py:33
  116.9 1.0 broadcast_divide_fusion.1
  119.2 4.6 %collective-permute-start.4 = (f32[12,3,1,128]{3,0,2,1:T(8,128)}, f32[12,3,1,128]{3,0,2,1:T(8,128)}, u32[]{:S(2)}, u32[]{:S(2)}) collective-permute-start(f32[12,3,1,128]{3,0,2,1:T(8,128)} %get-tuple-element.14), channel_id=1, source_target_pairs={{0,256},{16,272},{32,288},{48,304},{64,320},{80,336},{96,352},{112... | collective-permute-start | bytes 55304 | tf_op jit(solution)/shard_map/ppermute | solution.py:10
  123.8 5.3 %collective-permute-start.7 = (f32[12,3,1,128]{3,0,2,1:T(8,128)}, f32[12,3,1,128]{3,0,2,1:T(8,128)}, u32[]{:S(2)}, u32[]{:S(2)}) collective-permute-start(f32[12,3,1,128]{3,0,2,1:T(8,128)} %get-tuple-element.15), channel_id=1, source_target_pairs={{0,4},{4,8},{8,12},{1,5},{5,9},{9,13},{2,6},{6,10},{10,14},{3,7},{... | collective-permute-start | bytes 55304 | tf_op jit(solution)/shard_map/ppermute | solution.py:26
  129.1 1.9 collective-permute-start.5
  131.7 3.1 %collective-permute-start.2 = (f32[12,3,32,1]{2,3,1,0:T(1,128)S(1)}, f32[12,3,32,1]{2,3,1,0:T(1,128)S(1)}, u32[]{:S(2)}, u32[]{:S(2)}) collective-permute-start(f32[12,3,32,1]{2,3,1,0:T(1,128)S(1)} %copy.45), channel_id=1, source_target_pairs={{0,16},{16,32},{32,48},{48,64},{64,80},{80,96},{96,112},{112,128},... | collective-permute-start | bytes 13832 | tf_op jit(solution)/shard_map/ppermute | solution.py:26
  134.8 5.7 %collective-permute-start = (f32[12,3,32,1]{2,3,1,0:T(1,128)S(1)}, f32[12,3,32,1]{2,3,1,0:T(1,128)S(1)}, u32[]{:S(2)}, u32[]{:S(2)}) collective-permute-start(f32[12,3,32,1]{2,3,1,0:T(1,128)S(1)} %copy.43), channel_id=1, source_target_pairs={{16,0},{32,16},{48,32},{64,48},{80,64},{96,80},{112,96},{128,112},... | collective-permute-start | bytes 13832 | tf_op jit(solution)/shard_map/ppermute | solution.py:27
  142.1 2.3 %multiply_reduce_fusion = (f32[12,32,128]{2,0,1:T(8,128)}, f32[12,3,32,128]{3,0,2,1:T(8,128)S(1)}) fusion(f32[3,32,128]{2,1,0:T(8,128)S(1)} %copy-done.1, f32[3,32,128]{2,1,0:T(8,128)S(1)} %bitcast.53, f32[12,3,32,128]{3,0,2,1:T(8,128)S(1)} %fusion.35, f32[12,3,1,128]{3,0,2,1:T(8,128)} %collective-permute-done.7, pred[32]{0:T(512)(128)(4,1)} %copy-done.5, ...), kind=kLoop, calls=%fused_computation.50 | loop fusion | flops 3047424 | bytes 1735744 | tf_op jit(solution)/shard_map/reduce_sum | solution.py:110
  144.5 52.8 %all-reduce.5.cloned.1.call-done = f32[12,32,128]{2,0,1:T(8,128)} async-done(((f32[12,32,128]{2,0,1:T(8,128)}), f32[12,32,128]{2,0,1:T(8,128)}) %all-reduce.5.cloned.1.call-update) | async-done | bytes 196624 | tf_op jit(solution)/shard_map/psum | solution.py:33
  197.2 1.0 broadcast_divide_fusion
  198.4 4.6 %collective-permute-start.10 = (f32[12,3,1,128]{3,0,2,1:T(8,128)S(1)}, f32[12,3,1,128]{3,0,2,1:T(8,128)S(1)}, u32[]{:S(2)}, u32[]{:S(2)}) collective-permute-start(f32[12,3,1,128]{3,0,2,1:T(8,128)S(1)} %get-tuple-element.7), channel_id=1, source_target_pairs={{0,256},{16,272},{32,288},{48,304},{64,320},{80,336},{96,352},{112... | collective-permute-start | bytes 55304 | tf_op jit(solution)/shard_map/ppermute | solution.py:10
  202.9 5.3 %collective-permute-start.12 = (f32[12,3,1,128]{3,0,2,1:T(8,128)S(1)}, f32[12,3,1,128]{3,0,2,1:T(8,128)S(1)}, u32[]{:S(2)}, u32[]{:S(2)}) collective-permute-start(f32[12,3,1,128]{3,0,2,1:T(8,128)S(1)} %get-tuple-element.8), channel_id=1, source_target_pairs={{0,4},{4,8},{8,12},{1,5},{5,9},{9,13},{2,6},{6,10},{10,14},{3,7},{... | collective-permute-start | bytes 55304 | tf_op jit(solution)/shard_map/ppermute | solution.py:26
  208.2 1.9 collective-permute-start.11
  210.8 5.1 %collective-permute-start.8 = (f32[12,3,32,1]{2,3,1,0:T(1,128)S(1)}, f32[12,3,32,1]{2,3,1,0:T(1,128)S(1)}, u32[]{:S(2)}, u32[]{:S(2)}) collective-permute-start(f32[12,3,32,1]{2,3,1,0:T(1,128)S(1)} %copy.49), channel_id=1, source_target_pairs={{16,0},{32,16},{48,32},{64,48},{80,64},{96,80},{112,96},{128,112},... | collective-permute-start | bytes 13832 | tf_op jit(solution)/shard_map/ppermute | solution.py:27
  216.2 1.9 collective-permute-start.9
  218.5 5.5 %collective-permute-done.9 = f32[12,3,32,1]{2,3,1,0:T(1,128)S(1)} collective-permute-done((f32[12,3,32,1]{2,3,1,0:T(1,128)S(1)}, f32[12,3,32,1]{2,3,1,0:T(1,128)S(1)}, u32[]{:S(2)}, u32[]{:S(2)}) %collective-permute-start.9) | collective-permute-done | bytes 4640 | tf_op jit(solution)/shard_map/ppermute | solution.py:26
  224.5 0.8 fusion.7
  225.2 1.0 copy.53
  (84 shorter events, 9.9 us)
Async XLA Ops:
  7.2 46.5 %collective-permute-start.6 = (f32[3,1,128]{2,0,1:T(4,128)S(1)}, f32[3,1,128]{2,0,1:T(4,128)S(1)}, u32[]{:S(2)}, u32[]{:S(2)}) collective-permute-start(f32[3,1,128]{2,0,1:T(4,128)S(1)} %copy.79), channel_id=1, source_target_pairs={{0,4},{4,8},{8,12},{1,5},{5,9},{9,13},{2,6},{6,10},{10,14},{3,7},{... | collective-permute-start | bytes 4616 | tf_op jit(solution)/shard_map/ppermute | solution.py:16
  13.3 40.5 %collective-permute-start.3 = (f32[2,3,128]{2,1,0:T(4,128)S(1)}, f32[2,3,128]{2,1,0:T(4,128)S(1)}, u32[]{:S(2)}, u32[]{:S(2)}) collective-permute-start(f32[2,3,128]{2,1,0:T(4,128)S(1)} %pad_maximum_fusion.8), channel_id=1, source_target_pairs={{0,256},{16,272},{32,288},{48,304},{64,320},{80,336},{96,352},{112... | collective-permute-start | bytes 9224 | tf_op jit(solution)/shard_map/ppermute | solution.py:10
  18.8 34.8 %collective-permute-start.1 = (f32[3,32,1]{2,1,0:T(8,128)S(1)}, f32[3,32,1]{2,1,0:T(8,128)S(1)}, u32[]{:S(2)}, u32[]{:S(2)}) collective-permute-start(f32[3,32,1]{2,1,0:T(8,128)S(1)} %slice.98), channel_id=1, source_target_pairs={{0,16},{16,32},{32,48},{48,64},{64,80},{80,96},{96,112},{112,128},... | collective-permute-start | bytes 1160 | tf_op jit(solution)/shard_map/ppermute | solution.py:10
  28.4 8.7 %copy-start.2 = (f32[3,32,128]{2,1,0:T(8,128)S(1)}, f32[3,32,128]{2,1,0:T(8,128)}, u32[]{:S(2)}) copy-start(f32[3,32,128]{2,1,0:T(8,128)} %param.11) | copy-start | bytes 147460
  28.4 8.8 %copy-start.3 = (f32[3,32,128]{2,1,0:T(8,128)S(1)}, f32[3,32,128]{2,1,0:T(8,128)}, u32[]{:S(2)}) copy-start(f32[3,32,128]{2,1,0:T(8,128)} %param.14) | copy-start | bytes 147460
  28.4 8.8 %copy-start.1 = (f32[3,32,128]{2,1,0:T(8,128)S(1)}, f32[3,32,128]{2,1,0:T(8,128)}, u32[]{:S(2)}) copy-start(f32[3,32,128]{2,1,0:T(8,128)} %param.15) | copy-start | bytes 147460
  28.4 25.4 %copy-start.4 = (f32[3,32,128]{2,1,0:T(8,128)S(1)}, f32[3,32,128]{2,1,0:T(8,128)}, u32[]{:S(2)}) copy-start(f32[3,32,128]{2,1,0:T(8,128)} %param.12) | copy-start | bytes 147460
  28.4 27.6 %all-to-all-start = ((f32[128,2,4,4]{3,1,2,0:T(2,128)}), f32[128,2,4,4]{3,1,2,0:T(2,128)S(1)}, u32[]{:S(2)}, u32[]{:S(2)}) async-start(f32[128,2,4,4]{3,1,2,0:T(2,128)} %copy.40), calls=%async_computation | async-start | bytes 1048576 | tf_op jit(solution)/shard_map/all_to_all | solution.py:76
  37.1 79.8 %all-reduce.3.cloned.1.call-start = ((), (), s32[]{:S(2)}) async-start(), calls=%async_computation.1 | async-start | bytes 524288 | tf_op jit(solution)/shard_map/psum | solution.py:33
  37.2 24.0 %copy-start.7 = (pred[32]{0:T(512)(128)(4,1)}, pred[32]{0:T(512)(128)(4,1)S(1)}, u32[]{:S(2)}) copy-start(pred[32]{0:T(512)(128)(4,1)S(1)} %get-tuple-element.22) | copy-start | bytes 100
  37.2 103.3 %copy-start.5 = (pred[32]{0:T(512)(128)(4,1)}, pred[32]{0:T(512)(128)(4,1)S(1)}, u32[]{:S(2)}) copy-start(pred[32]{0:T(512)(128)(4,1)S(1)} %get-tuple-element.21) | copy-start | bytes 100
  56.4 4.8 %copy-start = (f32[12,3,32,128]{3,2,1,0:T(8,128)S(1)}, f32[12,3,32,128]{3,2,1,0:T(8,128)}, u32[]{:S(2)}) copy-start(f32[12,3,32,128]{3,2,1,0:T(8,128)} %param.10) | copy-start | bytes 1769476
  61.2 1.2 copy-start.9
  62.4 134.8 %all-reduce.5.cloned.1.call-start = ((), (), s32[]{:S(2)}) async-start(), calls=%async_computation.2 | async-start | bytes 524288 | tf_op jit(solution)/shard_map/psum | solution.py:33
  119.2 22.8 %collective-permute-start.4 = (f32[12,3,1,128]{3,0,2,1:T(8,128)}, f32[12,3,1,128]{3,0,2,1:T(8,128)}, u32[]{:S(2)}, u32[]{:S(2)}) collective-permute-start(f32[12,3,1,128]{3,0,2,1:T(8,128)} %get-tuple-element.14), channel_id=1, source_target_pairs={{0,256},{16,272},{32,288},{48,304},{64,320},{80,336},{96,352},{112... | collective-permute-start | bytes 55304 | tf_op jit(solution)/shard_map/ppermute | solution.py:10
  123.8 18.2 %collective-permute-start.7 = (f32[12,3,1,128]{3,0,2,1:T(8,128)}, f32[12,3,1,128]{3,0,2,1:T(8,128)}, u32[]{:S(2)}, u32[]{:S(2)}) collective-permute-start(f32[12,3,1,128]{3,0,2,1:T(8,128)} %get-tuple-element.15), channel_id=1, source_target_pairs={{0,4},{4,8},{8,12},{1,5},{5,9},{9,13},{2,6},{6,10},{10,14},{3,7},{... | collective-permute-start | bytes 55304 | tf_op jit(solution)/shard_map/ppermute | solution.py:26
  129.1 12.9 %collective-permute-start.5 = (f32[12,3,1,128]{3,0,2,1:T(8,128)}, f32[12,3,1,128]{3,0,2,1:T(8,128)}, u32[]{:S(2)}, u32[]{:S(2)}) collective-permute-start(f32[12,3,1,128]{3,0,2,1:T(8,128)} %get-tuple-element.16), channel_id=1, source_target_pairs={{4,0},{8,4},{12,8},{5,1},{9,5},{13,9},{6,2},{10,6},{14,10},{7,3},{... | collective-permute-start | bytes 55304 | tf_op jit(solution)/shard_map/ppermute | solution.py:27
  131.7 9.9 %collective-permute-start.2 = (f32[12,3,32,1]{2,3,1,0:T(1,128)S(1)}, f32[12,3,32,1]{2,3,1,0:T(1,128)S(1)}, u32[]{:S(2)}, u32[]{:S(2)}) collective-permute-start(f32[12,3,32,1]{2,3,1,0:T(1,128)S(1)} %copy.45), channel_id=1, source_target_pairs={{0,16},{16,32},{32,48},{48,64},{64,80},{80,96},{96,112},{112,128},... | collective-permute-start | bytes 13832 | tf_op jit(solution)/shard_map/ppermute | solution.py:26
  134.8 6.4 %collective-permute-start = (f32[12,3,32,1]{2,3,1,0:T(1,128)S(1)}, f32[12,3,32,1]{2,3,1,0:T(1,128)S(1)}, u32[]{:S(2)}, u32[]{:S(2)}) collective-permute-start(f32[12,3,32,1]{2,3,1,0:T(1,128)S(1)} %copy.43), channel_id=1, source_target_pairs={{16,0},{32,16},{48,32},{64,48},{80,64},{96,80},{112,96},{128,112},... | collective-permute-start | bytes 13832 | tf_op jit(solution)/shard_map/ppermute | solution.py:27
  198.4 26.1 %collective-permute-start.10 = (f32[12,3,1,128]{3,0,2,1:T(8,128)S(1)}, f32[12,3,1,128]{3,0,2,1:T(8,128)S(1)}, u32[]{:S(2)}, u32[]{:S(2)}) collective-permute-start(f32[12,3,1,128]{3,0,2,1:T(8,128)S(1)} %get-tuple-element.7), channel_id=1, source_target_pairs={{0,256},{16,272},{32,288},{48,304},{64,320},{80,336},{96,352},{112... | collective-permute-start | bytes 55304 | tf_op jit(solution)/shard_map/ppermute | solution.py:10
  202.9 21.5 %collective-permute-start.12 = (f32[12,3,1,128]{3,0,2,1:T(8,128)S(1)}, f32[12,3,1,128]{3,0,2,1:T(8,128)S(1)}, u32[]{:S(2)}, u32[]{:S(2)}) collective-permute-start(f32[12,3,1,128]{3,0,2,1:T(8,128)S(1)} %get-tuple-element.8), channel_id=1, source_target_pairs={{0,4},{4,8},{8,12},{1,5},{5,9},{9,13},{2,6},{6,10},{10,14},{3,7},{... | collective-permute-start | bytes 55304 | tf_op jit(solution)/shard_map/ppermute | solution.py:26
  208.2 16.2 %collective-permute-start.11 = (f32[12,3,1,128]{3,0,2,1:T(8,128)S(1)}, f32[12,3,1,128]{3,0,2,1:T(8,128)S(1)}, u32[]{:S(2)}, u32[]{:S(2)}) collective-permute-start(f32[12,3,1,128]{3,0,2,1:T(8,128)S(1)} %get-tuple-element.9), channel_id=1, source_target_pairs={{4,0},{8,4},{12,8},{5,1},{9,5},{13,9},{6,2},{10,6},{14,10},{7,3},{... | collective-permute-start | bytes 55304 | tf_op jit(solution)/shard_map/ppermute | solution.py:27
  210.8 7.3 %collective-permute-start.8 = (f32[12,3,32,1]{2,3,1,0:T(1,128)S(1)}, f32[12,3,32,1]{2,3,1,0:T(1,128)S(1)}, u32[]{:S(2)}, u32[]{:S(2)}) collective-permute-start(f32[12,3,32,1]{2,3,1,0:T(1,128)S(1)} %copy.49), channel_id=1, source_target_pairs={{16,0},{32,16},{48,32},{64,48},{80,64},{96,80},{112,96},{128,112},... | collective-permute-start | bytes 13832 | tf_op jit(solution)/shard_map/ppermute | solution.py:27
  216.2 8.3 %copy-start.6 = (pred[32]{0:T(512)(128)(4,1)S(1)}, pred[32]{0:T(512)(128)(4,1)}, u32[]{:S(2)}) copy-start(pred[32]{0:T(512)(128)(4,1)} %copy-done.5) | copy-start | bytes 100
  216.2 8.3 %copy-start.8 = (pred[32]{0:T(512)(128)(4,1)S(1)}, pred[32]{0:T(512)(128)(4,1)}, u32[]{:S(2)}) copy-start(pred[32]{0:T(512)(128)(4,1)} %copy-done.7) | copy-start | bytes 100
  216.2 7.8 %collective-permute-start.9 = (f32[12,3,32,1]{2,3,1,0:T(1,128)S(1)}, f32[12,3,32,1]{2,3,1,0:T(1,128)S(1)}, u32[]{:S(2)}, u32[]{:S(2)}) collective-permute-start(f32[12,3,32,1]{2,3,1,0:T(1,128)S(1)} %copy.51), channel_id=1, source_target_pairs={{0,16},{16,32},{32,48},{48,64},{64,80},{80,96},{96,112},{112,128},... | collective-permute-start | bytes 13832 | tf_op jit(solution)/shard_map/ppermute | solution.py:26
Sparse Core Ops, SparseCore 0:
  62.5 54.2 all-reduce.2
  144.6 52.6 all-reduce.4
